TPU v7x, 32 devices: a whole 2x2x4 slice. The times are simulated.
32 devices in a mesh: groups: 2 (over y), seq: 4 (over z), tp: 4 (over x, core).
Axes of the slice: x: 2, y: 2, z: 4, core: 2. Of those that a mesh axis runs over, the one named last changes fastest.
Arguments:
- activations: bfloat16 [1024, 8192], P(('groups', 'seq'), 'tp'), parts along dimension 0, may hold values from -24 to 24
- queries: bfloat16 [1024, 8192], P(('groups', 'seq'), 'tp'), parts along dimension 0, may hold values from -24 to 24
- key_weight: bfloat16 [8192, 1024], P(None, 'tp'), may hold values from -0.0625 to 0.0625
- value_weight: bfloat16 [8192, 1024], P(None, 'tp'), may hold values from -0.0625 to 0.0625
- lengths: int32 [8], P('groups'), parts along dimension 0, may hold values from 1 to 320, 512 in all
- owners: int32 [32], P('groups'), parts along dimension 0, may hold values from 0 to 3, as said below
Outputs:
- attention: bfloat16 [1024, 8192], P(('groups', 'seq'), 'tp'), parts along dimension 0
- kv_cache: bfloat16 [1024, 8, 256], P(('groups', 'seq'), 'tp'), parts along dimension 0
There are 2 independent parts, one for each index of `groups`. A program takes and returns all parts, laid end to end along the dimension named above; an argument that names none is the same for every part. Nothing has to cross between parts.
Inputs may be any that keep to these rules, and one draw needn't show every extreme that they name: `owners`: every decode device is named by exactly 4 blocks; among the 4 blocks of the rows of one index of seq, no decode device is named more than 2 times, and some is named exactly 2 times.
All inputs are finite; a program needn't handle non-finite values.
Results may differ from a plain program's by a relative error of at most 0.0045.
The roundings to bfloat16 on the way count: a program that leaves them out, or rounds other values in their place, can miss the bound.
Values may be sent and summed in bfloat16 or wider, within the bound.
No kernel may reach another device: no remote copies, remote signals or barrier semaphores. Data moves between devices by JAX's collectives and lax.ppermute only.
A program may use at most 64 MiB of HBM per device.

v0:
```python
import jax
import jax.numpy as jnp
from jax import lax
from jax.sharding import PartitionSpec as P

HD = 128


def locate(row_ids, lengths):
    prompt_ends = jnp.cumsum(lengths)
    prompt_starts = prompt_ends - lengths
    segment = jnp.sum((row_ids[:, None] >= prompt_ends[None, :]).astype(jnp.int32), axis=1)
    numbers = jnp.arange(lengths.shape[0], dtype=jnp.int32)
    prompt_first = jnp.sum(
        jnp.where(segment[:, None] == numbers[None, :], prompt_starts[None, :], 0), axis=1
    )
    return (segment, row_ids - prompt_first)


def rotate(vectors, positions):
    half_size = vectors.shape[-1] // 2
    exponent = jnp.arange(half_size, dtype=jnp.float32) * (2.0 / vectors.shape[-1])
    inverse = jnp.exp(-exponent * jnp.log(jnp.float32(500000.0)))
    angles = positions.astype(jnp.float32)[:, None] * inverse[None, :]
    cosines = jnp.cos(angles)[:, None, :]
    sine_values = jnp.sin(angles)[:, None, :]
    lower_half = vectors[..., :half_size]
    upper_half = vectors[..., half_size:]
    return jnp.concatenate(
        [
            lower_half * cosines - upper_half * sine_values,
            upper_half * cosines + lower_half * sine_values,
        ],
        axis=-1,
    )


def per_device(activations, queries, key_weight, value_weight, lengths, owners):
    local_rows = activations.shape[0]
    devices = lax.axis_size("seq")
    own_index = lax.axis_index("seq")
    kv_width = key_weight.shape[1]
    kv_heads = kv_width // HD
    query_heads = queries.shape[1] // HD
    group_size = query_heads // kv_heads
    row_ids = own_index * local_rows + jnp.arange(local_rows, dtype=jnp.int32)
    segment, positions = locate(row_ids, lengths)
    portion = lax.all_gather(activations, "tp", axis=1, tiled=True)
    key_rows = key_weight
    key_sums = jnp.dot(portion, key_rows, preferred_element_type=jnp.float32)
    value_sums = jnp.dot(portion, value_weight, preferred_element_type=jnp.float32)
    keys_local = rotate(key_sums.reshape(local_rows, kv_heads, HD), positions).astype(jnp.bfloat16)
    values_local = value_sums.astype(jnp.bfloat16).reshape(local_rows, kv_heads, HD)
    packed = jnp.concatenate([keys_local, values_local], axis=-1).reshape(
        local_rows, kv_heads * 2 * HD
    )
    rotated = rotate(queries.astype(jnp.float32).reshape(local_rows, query_heads, HD), positions)
    rotated = rotated.astype(jnp.bfloat16).reshape(local_rows, kv_heads, group_size, HD)

    def attend_block(running, portion, offset):
        running_max, running_sum, running_out = running
        amount = portion.shape[0]
        paired = portion.reshape(amount, kv_heads, 2 * HD)
        key_part = paired[:, :, :HD]
        value_part = paired[:, :, HD:]
        key_rows = offset + jnp.arange(amount, dtype=jnp.int32)
        key_segment, unused = locate(key_rows, lengths)
        allowed = (
            (key_segment[None, :] == segment[:, None])
            & (key_rows[None, :] <= row_ids[:, None])
            & (key_rows[None, :] >= 0)
        )
        allowed = allowed[:, None, None, :]
        scores = jnp.einsum(
            "qhgd,khd->qhgk", rotated, key_part, preferred_element_type=jnp.float32
        ) / jnp.sqrt(jnp.float32(HD))
        new_max = jnp.maximum(running_max, jnp.max(jnp.where(allowed, scores, -1e30), axis=-1))
        weights = jnp.where(allowed, jnp.exp(scores - new_max[..., None]), 0.0)
        factor = jnp.exp(running_max - new_max)
        running_sum = running_sum * factor + jnp.sum(weights, axis=-1)
        running_out = running_out * factor[..., None] + jnp.einsum(
            "qhgk,khd->qhgd",
            weights.astype(jnp.bfloat16),
            value_part,
            preferred_element_type=jnp.float32,
        )
        return (new_max, running_sum, running_out)

    def attend(running, portion, offset):
        amount = portion.shape[0]
        if amount > 512 and amount % 512 == 0:

            def advance(carried, entry):
                sub_portion, sub_offset = entry
                return (attend_block(carried, sub_portion, offset + sub_offset), None)

            offsets = jnp.arange(amount // 512, dtype=jnp.int32) * 512
            running, unused = lax.scan(
                advance, running, (portion.reshape(amount // 512, 512, portion.shape[1]), offsets)
            )
            return running
        return attend_block(running, portion, offset)

    initial = (
        jnp.full((local_rows, kv_heads, group_size), -1e30, jnp.float32),
        jnp.zeros((local_rows, kv_heads, group_size), jnp.float32),
        jnp.zeros((local_rows, kv_heads, group_size, HD), jnp.float32),
    )
    blocks_dev = owners.shape[0] // devices
    block_len = local_rows // blocks_dev
    is_own = owners == own_index
    ordinal = jnp.cumsum(is_own.astype(jnp.int32)) - 1
    matches = is_own[None, :] & (
        ordinal[None, :] == jnp.arange(blocks_dev, dtype=jnp.int32)[:, None]
    )
    leading = jnp.sum(
        jnp.where(matches, jnp.arange(owners.shape[0], dtype=jnp.int32)[None, :], 0), axis=1
    )
    within = jnp.arange(local_rows, dtype=jnp.int32)
    wanted = jnp.repeat(leading, block_len) * block_len + within % block_len
    portion = lax.all_gather(packed, "seq", axis=0, tiled=True)
    amount = portion.shape[0]
    choose = (wanted[:, None] == jnp.arange(amount, dtype=jnp.int32)[None, :]).astype(jnp.bfloat16)
    running = attend(
        (initial, jnp.zeros((local_rows, packed.shape[1]), jnp.float32))[0], portion, jnp.int32(0)
    )
    taken = jnp.dot(choose, portion, preferred_element_type=jnp.float32)
    kv_cache = taken.astype(jnp.bfloat16).reshape(local_rows, kv_heads, 2 * HD)
    running_max, running_sum, running_out = running
    attention = (
        (running_out / running_sum[..., None])
        .astype(jnp.bfloat16)
        .reshape(local_rows, query_heads * HD)
    )
    return (attention, kv_cache)


def solution(mesh):
    in_specs = (
        P(("groups", "seq"), "tp"),
        P(("groups", "seq"), "tp"),
        P(None, "tp"),
        P(None, "tp"),
        P("groups"),
        P("groups"),
    )
    out_specs = (P(("groups", "seq"), "tp"), P(("groups", "seq"), "tp", None))
    return jax.shard_map(
        per_device, mesh=mesh, in_specs=in_specs, out_specs=out_specs, check_vma=False
    )
```

profile of v0, /device:TPU:0, one launch (start us, length us, event | category | flops | bytes accessed | tf_op | source)
XLA Modules:
  0.0 71.7 jit_solution(17123226598475692947)
XLA Ops:
  7.2 0.0 copy-start.2
  7.2 0.0 copy-start.3
  7.2 0.0 all-gather.2.cloned.1.call-start
  7.2 0.7 all-gather.2.cloned.1.call-update
  7.9 1.1 %convert_bitcast_fusion = f32[16,8,16,128]{3,1,2,0:T(8,128)S(1)} fusion(bf16[128,2048]{1,0:T(8,128)(2,1)} %param.7), kind=kLoop, calls=%fused_computation.16 | loop fusion | flops 262144 | bytes 1572864
  9.1 0.2 copy.34
  9.3 0.0 copy-done.2
  9.3 0.1 copy.26
  9.4 0.0 copy-done.3
  9.4 0.2 reduce-window.16
  9.6 0.1 add_reduce_fusion
  9.7 0.1 select_reduce_fusion
  9.8 0.1 broadcast_in_dim.57
  9.9 0.1 mul.144
  10.0 0.1 convert_reduce_fusion
  10.1 0.1 convert_reduce_fusion.1
  10.2 0.1 select_reduce_fusion.1
  10.3 0.1 fusion.23
  10.4 0.3 multiply_cosine_fusion
  10.7 0.3 fusion.31
  11.1 0.7 subtract_convert_fusion
  11.8 23.1 %all-gather.2.cloned.1.call-done = bf16[128,8192]{1,0:T(8,128)(2,1)} async-done(((bf16[128,2048]{1,0:T(8,128)(2,1)}), bf16[128,8192]{1,0:T(8,128)(2,1)}) %all-gather.2.cloned.1.call-update) | async-done | bytes 2097168 | tf_op jit(solution)/shard_map/all_gather | solution.py:48
  34.9 0.0 copy-start
  34.9 4.3 %fusion.32 = f32[128,256]{1,0:T(8,128)} fusion(bf16[128,8192]{1,0:T(8,128)(2,1)} %all-gather.2.cloned.1.call-done, bf16[8192,256]{1,0:T(8,128)(2,1)} %param.8), kind=kOutput, calls=%fused_computation.60 | convolution fusion | flops 536870912 | bytes 6422528 | tf_op jit(solution)/shard_map/dot_general | solution.py:50
  39.2 1.0 %reshape.227 = f32[128,2,128]{2,1,0:T(2,128)S(1)} reshape(f32[128,256]{1,0:T(8,128)} %fusion.32) | data formatting | bytes 262144 | tf_op jit(solution)/shard_map/reshape | solution.py:52
  40.2 0.9 %subtract_convert_fusion.1 = (bf16[128,2,64]{2,1,0:T(2,128)(2,1)S(1)}, bf16[128,2,64]{2,1,0:T(2,128)(2,1)}) fusion(f32[128,2,128]{2,1,0:T(2,128)S(1)} %reshape.227, f32[128,64]{1,0:T(8,128)S(1)} %get-tuple-element.19, f32[128,64]{1,0:T(8,128)S(1)} %get-tuple-element.18), kind=kLoop, calls=%fused_computation.32 | loop fusion | flops 131072 | bytes 262144 | tf_op jit(solution)/shard_map/convert.6
  41.1 0.0 copy-done
  41.1 0.0 copy-start.1
  41.1 2.9 %convolution_convert_fusion.1 = bf16[128,256]{1,0:T(8,128)(2,1)S(1)} fusion(bf16[128,8192]{1,0:T(8,128)(2,1)S(1)} %copy-done, bf16[8192,256]{1,0:T(8,128)(2,1)} %param.9), kind=kOutput, calls=%fused_computation.15 | convolution fusion | flops 536903680 | bytes 6356992 | tf_op jit(solution)/shard_map/dot_general | solution.py:51
  44.0 0.0 copy-done.1
  44.0 0.3 pad_maximum_fusion
  44.3 0.1 copy.21
  44.5 15.3 %all_gather.7 = bf16[512,512]{0,1:T(8,128)(2,1)S(1)} all-gather(bf16[128,512]{0,1:T(8,128)(2,1)S(1)} %bitcast.62), channel_id=1, replica_groups=mesh['groups'=2,'seq'=4,'tp'=4] {'seq'}, dimensions={0}, use_global_device_ids=true | all-gather | bytes 655360 | tf_op jit(solution)/shard_map/all_gather | solution.py:121
  59.8 1.1 %fusion = (f32[128,2,8]{0,2,1:T(8,128)S(1)}, f32[2,512,128,8]{2,1,3,0:T(8,128)S(1)}) fusion(pred[128,512]{0,1:T(8,128)(4,1)S(1)} %fusion.23, bf16[128,2,8,64]{3,0,2,1:T(8,128)(2,1)S(1)} %bitcast.61, bf16[128,2,8,64]{3,0,2,1:T(8,128)(2,1)S(1)} %bitcast.60, bf16[512,2,256]{0,2,1:T(8,128)(2,1)S(1)} %bitcast.58), kind=kOutput, calls=%fused_computation.2 | convolution fusion | flops 272627712 | bytes 5578752 | tf_op jit(solution)/shard_map/qhgd,khd->qhgk/dot_general | solution.py:74
  60.9 0.9 %fusion.3 = f32[128,2,8]{0,2,1:T(8,128)S(1)} fusion(f32[2,512,128,8]{2,1,3,0:T(8,128)S(1)} %get-tuple-element.21, f32[128,2,8]{0,2,1:T(8,128)S(1)} %broadcast_maximum_fusion, pred[128,512]{0,1:T(8,128)(4,1)S(1)} %fusion.23), kind=kLoop, calls=%fused_computation.5 | loop fusion | flops 4192256 | bytes 4276224 | tf_op jit(solution)/shard_map/reduce_sum | solution.py:80
  61.8 1.0 %divide_convert_fusion = bf16[128,2,8,128]{0,3,2,1:T(8,128)(2,1)S(1)} fusion(f32[2,512,128,8]{2,1,3,0:T(8,128)S(1)} %get-tuple-element.21, f32[128,2,8]{0,2,1:T(8,128)S(1)} %broadcast_maximum_fusion, pred[128,512]{0,1:T(8,128)(4,1)S(1)} %fusion.23, f32[128,2,8]{0,2,1:T(8,128)S(1)} %get-tuple-element.17, f32[128,2,8]{0,2,1:T(8,128)S(1)} %get-tuple-element.16, ...), kind=kOutput, calls=%fused_computation.17 | convolution fusion | flops 273416192 | bytes 5070848 | tf_op jit(solution)/shard_map/qhgk,khd->qhgd/dot_general | solution.py:81
  62.8 1.0 %copy.27 = bf16[128,2048]{1,0:T(8,128)(2,1)} copy(bf16[128,2048]{0,1:T(8,128)(2,1)S(1)} %bitcast.63) | data formatting | bytes 1048576
  63.8 0.3 convolution_convert_fusion
  64.1 0.7 reshape.235
  (11 shorter events, 0.1 us)
Async XLA Ops:
  7.2 2.1 %copy-start.2 = (s32[16]{0:T(128)S(1)}, s32[16]{0:T(128)}, u32[]{:S(2)}) copy-start(s32[16]{0:T(128)} %param.11) | copy-start | bytes 196
  7.2 2.2 %copy-start.3 = (s32[4]{0:T(128)S(1)}, s32[4]{0:T(128)}, u32[]{:S(2)}) copy-start(s32[4]{0:T(128)} %param.10) | copy-start | bytes 52
  7.2 27.7 %all-gather.2.cloned.1.call-start = ((), (), s32[]{:S(2)}) async-start(), calls=%async_computation | async-start | bytes 2621440 | tf_op jit(solution)/shard_map/all_gather | solution.py:48
  34.9 6.2 %copy-start = (bf16[128,8192]{1,0:T(8,128)(2,1)S(1)}, bf16[128,8192]{1,0:T(8,128)(2,1)}, u32[]{:S(2)}) copy-start(bf16[128,8192]{1,0:T(8,128)(2,1)} %all-gather.2.cloned.1.call-done) | copy-start | bytes 6291460
  41.1 3.0 %copy-start.1 = (bf16[128,2,64]{2,1,0:T(2,128)(2,1)S(1)}, bf16[128,2,64]{2,1,0:T(2,128)(2,1)}, u32[]{:S(2)}) copy-start(bf16[128,2,64]{2,1,0:T(2,128)(2,1)} %get-tuple-element.15) | copy-start | bytes 98308
Sparse Core Ops, SparseCore 0:
  9.6 25.2 all-gather.1
where the time goes:
time: 71.9 us; the launch traced here: 71.7 us
  waiting for transfers between devices  23.8 us (33%)
  blocking collectives  15.3 us (21%)
  between operations  14.2 us (20%)
  matrix products  9.66 us (13%)
  other arithmetic  5.07 us (7%)
  local copies, waits for them, and re-layouts  3.61 us (5%)
    all_gather x1, waiting for transfers between devices, per_device(): portion = lax.all_gather(activations, 'tp', axis=1, tiled=True)  23.1 us
    all_gather x1, blocking collectives, per_device(): portion = lax.all_gather(packed, 'seq', axis=0, tiled=True)  15.3 us
    dot_general x1, matrix products, per_device(): key_sums = jnp.dot(portion, key_rows, preferred_element_type=jnp.float32)  4.34 us
    dot_general x1, matrix products, per_device(): jnp.dot(portion, value_weight, preferred_element_type=jnp.float32)  2.93 us
    another operation x5, other arithmetic  1.78 us
  transfers between devices with their start and end apart: 1, of which 1 were waited for; matrix products, arithmetic and copies ran while one was open for 5% of the time, Pallas kernels for 0%

commit v1 on v0

--- a/solution.py
+++ b/solution.py
@@ -45,7 +45,13 @@
     group_size = query_heads // kv_heads
     row_ids = own_index * local_rows + jnp.arange(local_rows, dtype=jnp.int32)
     segment, positions = locate(row_ids, lengths)
-    portion = lax.all_gather(activations, "tp", axis=1, tiled=True)
+    devices_2 = lax.axis_size("tp")
+    current, blocks = (activations, [activations])
+    for _ in range(devices_2 - 1):
+        current = lax.ppermute(current, "tp", [(i, (i + 1) % devices_2) for i in range(devices_2)])
+        blocks.insert(0, current)
+    line = jnp.concatenate(blocks, axis=1)
+    portion = jnp.roll(line, (lax.axis_index("tp") + 1) * activations.shape[1], axis=1)
     key_rows = key_weight
     key_sums = jnp.dot(portion, key_rows, preferred_element_type=jnp.float32)
     value_sums = jnp.dot(portion, value_weight, preferred_element_type=jnp.float32)

time: 71.9 us -> 55.7 us (0.77)
  between operations: 14.2 us -> 0.86 us
  waiting for transfers between devices: 23.8 us -> 20.3 us
  matrix products: 9.66 us -> 6.63 us
  other arithmetic: 5.07 us -> 6.44 us
  local copies, waits for them, and re-layouts: 3.61 us -> 4.94 us
    all_gather x1 -> x0, waiting for transfers between devices: 23.1 us -> none  [per_device(): portion = lax.all_gather(activations, 'tp', axis=1, tiled=True)]
    ppermute x0 -> x3, waiting for transfers between devices: none -> 20.3 us  [per_device(): lax.ppermute(current, 'tp', [(i, (i + 1) % devices_2) for i in range(devi...]
    dot_general x1, matrix products: 4.34 us -> 0.71 us  [per_device(): key_sums = jnp.dot(portion, key_rows, preferred_element_type=jnp.float32)]
    unnamed x10 -> x15, local copies, waits for them, and re-layouts: 1.21 us -> 3.4 us
    reshape x1, local copies, waits for them, and re-layouts: 0.97 us -> 0.07 us  [per_device(): key_sums.reshape(local_rows, kv_heads, HD)]
    another operation x5, other arithmetic: 1.78 us -> 2.51 us
  transfers between devices with their start and end apart: 1 -> 3, of which waited for: 1 -> 3; matrix products, arithmetic and copies ran while one was open for 5% -> 10% of each run, Pallas kernels for 0% -> 0%
where the time goes in v1:
time: 55.7 us; the launch traced here: 55.5 us
  waiting for transfers between devices  20.3 us (36%)
  blocking collectives  15.7 us (28%)
  matrix products  6.63 us (12%)
  other arithmetic  6.44 us (12%)
  local copies, waits for them, and re-layouts  4.94 us (9%)
  between operations  0.86 us (2%)
  starting transfers between devices  0.59 us (1%)
    ppermute x3, waiting for transfers between devices, per_device(): lax.ppermute(current, 'tp', [(i, (i + 1) % devices_2) for i in range(devi...  20.3 us
    all_gather x1, blocking collectives, per_device(): portion = lax.all_gather(packed, 'seq', axis=0, tiled=True)  15.7 us
    dot_general x1, matrix products, per_device(): jnp.dot(portion, value_weight, preferred_element_type=jnp.float32)  3.54 us
    unnamed x15, local copies, waits for them, and re-layouts  3.4 us
    another operation x5, other arithmetic  2.51 us
    unnamed x1, other arithmetic  1.14 us
  transfers between devices with their start and end apart: 3, of which 3 were waited for; matrix products, arithmetic and copies ran while one was open for 10% of the time, Pallas kernels for 0%

profile of v1, /device:TPU:0, one launch (start us, length us, event | category | flops | bytes accessed | tf_op | source)
XLA Modules:
  0.0 55.5 jit_solution(5962415893519568963)
XLA Ops:
  0.6 0.5 collective-permute-start
  1.2 0.8 %reduce-window.16 = s32[4,1]{0,1:T(1,128)S(1)} reduce-window(s32[4,1]{0,1:T(1,128)} %bitcast.64, s32[]{:T(128)} %constant.63.clone.1), window={size=4x1 pad=3_0x0_0}, to_apply=%region_0.0 | reduce-window | flops 12 | bytes 36 | tf_op jit(solution)/shard_map/reduce-window.6
  2.0 0.7 %bitcast_subtract_fusion.1 = s32[4]{0:T(128)S(1)} fusion(s32[4]{0:T(128)} %param.10, s32[4,1]{0,1:T(1,128)S(1)} %reduce-window.16), kind=kLoop, calls=%fused_computation.69 | loop fusion | flops 4 | bytes 48 | tf_op jit(solution)/shard_map/sub | solution.py:11
  2.7 0.1 convert_reduce_fusion
  2.7 0.1 convert_reduce_fusion.1
  2.8 1.1 %convert_bitcast_fusion = f32[16,8,16,128]{3,1,2,0:T(8,128)S(1)} fusion(bf16[128,2048]{1,0:T(8,128)(2,1)} %param.7), kind=kLoop, calls=%fused_computation.20 | loop fusion | flops 262144 | bytes 1572864
  4.0 0.2 copy.34
  4.2 0.7 %convert_bitcast_fusion.1 = (s32[16,1]{0,1:T(1,128)S(1)}, pred[16]{0:T(512)(128)(4,1)S(1)}) fusion(s32[16]{0:T(128)} %param.11, s32[]{:T(128)S(6)} %axis_index.23), kind=kLoop, calls=%fused_computation.60 | loop fusion | flops 32 | bytes 148 | tf_op jit(solution)/shard_map/convert.1
  4.8 0.1 copy.26
  5.0 0.1 add_reduce_fusion
  5.1 0.1 select_reduce_fusion
  5.2 0.1 broadcast_in_dim.57
  5.3 0.1 mul.148
  5.4 0.1 select_reduce_fusion.1
  5.5 0.3 multiply_cosine_fusion
  5.8 4.4 %collective-permute-done = bf16[128,2048]{1,0:T(8,128)(2,1)S(1)} collective-permute-done((bf16[128,2048]{1,0:T(8,128)(2,1)}, bf16[128,2048]{1,0:T(8,128)(2,1)S(1)}, u32[]{:S(2)}, u32[]{:S(2)}) %collective-permute-start) | collective-permute-done | bytes 524320 | tf_op jit(solution)/shard_map/ppermute | solution.py:51
  10.2 0.0 collective-permute-start.1
  10.2 0.1 fusion.30
  10.3 0.3 fusion.40
  10.7 0.0 copy-start.2
  10.7 8.1 %collective-permute-done.1 = bf16[128,2048]{1,0:T(8,128)(2,1)S(1)} collective-permute-done((bf16[128,2048]{1,0:T(8,128)(2,1)S(1)}, bf16[128,2048]{1,0:T(8,128)(2,1)S(1)}, u32[]{:S(2)}, u32[]{:S(2)}) %collective-permute-start.1) | collective-permute-done | bytes 524320 | tf_op jit(solution)/shard_map/ppermute | solution.py:51
  18.8 0.0 collective-permute-start.2
  18.8 0.7 %subtract_convert_fusion = (bf16[128,16,64]{2,0,1:T(8,128)(2,1)S(1)}, bf16[128,16,64]{2,0,1:T(8,128)(2,1)S(1)}) fusion(f32[128,16,64]{2,1,0:T(8,128)S(1)} %get-tuple-element.13, f32[128,16,64]{2,1,0:T(8,128)S(1)} %get-tuple-element.12, f32[128,64]{1,0:T(8,128)S(1)} %get-tuple-element.19, f32[128,64]{1,0:T(8,128)S(1)} %get-tuple-element.18), kind=kLoop, calls=%fused_computation.23 | loop fusion | flops 1048576 | bytes 1638400 | tf_op jit(solution)/shard_map/convert.5
  19.5 0.0 copy-start.1
  19.5 7.9 %collective-permute-done.2 = bf16[128,2048]{1,0:T(8,128)(2,1)S(1)} collective-permute-done((bf16[128,2048]{1,0:T(8,128)(2,1)S(1)}, bf16[128,2048]{1,0:T(8,128)(2,1)S(1)}, u32[]{:S(2)}, u32[]{:S(2)}) %collective-permute-start.2) | collective-permute-done | bytes 524320 | tf_op jit(solution)/shard_map/ppermute | solution.py:51
  27.5 0.0 copy-done.2
  27.8 0.0 copy-start
  27.8 1.9 %copy-done = bf16[128,16384]{1,0:T(8,128)(2,1)} copy-done((bf16[128,16384]{1,0:T(8,128)(2,1)}, bf16[128,16384]{1,0:T(8,128)(2,1)S(1)}, u32[]{:S(2)}) %copy-start) | copy-done | bytes 4194328
  29.7 0.0 copy-done.1
  29.7 0.7 %fusion.13 = f32[128,256]{1,0:T(8,128)S(1)} fusion(bf16[8192,256]{1,0:T(8,128)(2,1)S(1)} %copy-done.1, bf16[128,16384]{1,0:T(8,128)(2,1)S(1)} %constant_dynamic-update-slice_fusion, s32[]{:T(128)S(6)} %select_n.39), kind=kOutput, calls=%fused_computation.14 | convolution fusion | flops 536870912 | bytes 6422532 | tf_op jit(solution)/shard_map/dot_general | solution.py:56
  30.4 0.1 reshape.227
  30.5 0.3 subtract_convert_fusion.1
  30.8 3.5 %fusion.21 = bf16[128,256]{1,0:T(8,128)(2,1)S(1)} fusion(bf16[8192,256]{1,0:T(8,128)(2,1)} %param.9, bf16[128,16384]{1,0:T(8,128)(2,1)} %copy-done, s32[]{:T(128)S(6)} %select_n.39), kind=kOutput, calls=%fused_computation.19 | convolution fusion | flops 536903680 | bytes 6356996 | tf_op jit(solution)/shard_map/dot_general | solution.py:57
  34.3 0.3 pad_maximum_fusion
  34.6 0.1 copy.21
  34.8 15.7 %all_gather.3 = bf16[512,512]{0,1:T(8,128)(2,1)S(1)} all-gather(bf16[128,512]{0,1:T(8,128)(2,1)S(1)} %bitcast.60), channel_id=1, replica_groups=mesh['groups'=2,'seq'=4,'tp'=4] {'seq'}, dimensions={0}, use_global_device_ids=true | all-gather | bytes 655360 | tf_op jit(solution)/shard_map/all_gather | solution.py:127
  50.5 1.1 %fusion = (f32[128,2,8]{0,2,1:T(8,128)S(1)}, f32[2,512,128,8]{2,1,3,0:T(8,128)S(1)}) fusion(pred[128,512]{0,1:T(8,128)(4,1)S(1)} %fusion.30, bf16[128,2,8,64]{3,0,2,1:T(8,128)(2,1)S(1)} %bitcast.59, bf16[128,2,8,64]{3,0,2,1:T(8,128)(2,1)S(1)} %bitcast.58, bf16[512,2,256]{0,2,1:T(8,128)(2,1)S(1)} %bitcast.56), kind=kOutput, calls=%fused_computation.2 | convolution fusion | flops 272627712 | bytes 5578752 | tf_op jit(solution)/shard_map/qhgd,khd->qhgk/dot_general | solution.py:80
  51.6 0.9 %fusion.3 = f32[128,2,8]{0,2,1:T(8,128)S(1)} fusion(f32[2,512,128,8]{2,1,3,0:T(8,128)S(1)} %get-tuple-element.21, f32[128,2,8]{0,2,1:T(8,128)S(1)} %broadcast_maximum_fusion, pred[128,512]{0,1:T(8,128)(4,1)S(1)} %fusion.30), kind=kLoop, calls=%fused_computation.5 | loop fusion | flops 4192256 | bytes 4276224 | tf_op jit(solution)/shard_map/reduce_sum | solution.py:86
  52.5 1.0 %divide_convert_fusion = bf16[128,2,8,128]{0,3,2,1:T(8,128)(2,1)S(1)} fusion(f32[2,512,128,8]{2,1,3,0:T(8,128)S(1)} %get-tuple-element.21, f32[128,2,8]{0,2,1:T(8,128)S(1)} %broadcast_maximum_fusion, pred[128,512]{0,1:T(8,128)(4,1)S(1)} %fusion.30, f32[128,2,8]{0,2,1:T(8,128)S(1)} %get-tuple-element.17, f32[128,2,8]{0,2,1:T(8,128)S(1)} %get-tuple-element.16, ...), kind=kOutput, calls=%fused_computation.21 | convolution fusion | flops 273416192 | bytes 5070848 | tf_op jit(solution)/shard_map/qhgk,khd->qhgd/dot_general | solution.py:87
  53.5 1.0 %copy.27 = bf16[128,2048]{1,0:T(8,128)(2,1)} copy(bf16[128,2048]{0,1:T(8,128)(2,1)S(1)} %bitcast.61) | data formatting | bytes 1048576
  54.5 0.3 convolution_convert_fusion
  54.8 0.7 %reshape.235 = bf16[128,2,256]{2,1,0:T(2,128)(2,1)} reshape(bf16[128,512]{1,0:T(8,128)(2,1)S(1)} %convolution_convert_fusion) | data formatting | bytes 262144 | tf_op jit(solution)/shard_map/reshape | solution.py:134
  (17 shorter events, 0.4 us)
Async XLA Ops:
  0.6 9.5 %collective-permute-start = (bf16[128,2048]{1,0:T(8,128)(2,1)}, bf16[128,2048]{1,0:T(8,128)(2,1)S(1)}, u32[]{:S(2)}, u32[]{:S(2)}) collective-permute-start(bf16[128,2048]{1,0:T(8,128)(2,1)} %param.6), channel_id=1, source_target_pairs={{0,1},{1,2},{2,3},{3,0},{4,5},{5,6},{6,7},{7,4},{8,9},{9,10},{10,1... | collective-permute-start | bytes 1572872 | tf_op jit(solution)/shard_map/ppermute | solution.py:51
  10.2 8.6 %collective-permute-start.1 = (bf16[128,2048]{1,0:T(8,128)(2,1)S(1)}, bf16[128,2048]{1,0:T(8,128)(2,1)S(1)}, u32[]{:S(2)}, u32[]{:S(2)}) collective-permute-start(bf16[128,2048]{1,0:T(8,128)(2,1)S(1)} %collective-permute-done), channel_id=1, source_target_pairs={{0,1},{1,2},{2,3},{3,0},{4,5},{5,6},{6,7},{7,4},{8,9},{9,10},{10,1... | collective-permute-start | bytes 1572872 | tf_op jit(solution)/shard_map/ppermute | solution.py:51
  10.7 16.8 %copy-start.2 = (bf16[128,2048]{1,0:T(8,128)(2,1)S(1)}, bf16[128,2048]{1,0:T(8,128)(2,1)}, u32[]{:S(2)}) copy-start(bf16[128,2048]{1,0:T(8,128)(2,1)} %param.6) | copy-start | bytes 1572868
  18.8 8.6 %collective-permute-start.2 = (bf16[128,2048]{1,0:T(8,128)(2,1)S(1)}, bf16[128,2048]{1,0:T(8,128)(2,1)S(1)}, u32[]{:S(2)}, u32[]{:S(2)}) collective-permute-start(bf16[128,2048]{1,0:T(8,128)(2,1)S(1)} %collective-permute-done.1), channel_id=1, source_target_pairs={{0,1},{1,2},{2,3},{3,0},{4,5},{5,6},{6,7},{7,4},{8,9},{9,10},{10,1... | collective-permute-start | bytes 1572872 | tf_op jit(solution)/shard_map/ppermute | solution.py:51
  19.5 10.2 %copy-start.1 = (bf16[8192,256]{1,0:T(8,128)(2,1)S(1)}, bf16[8192,256]{1,0:T(8,128)(2,1)}, u32[]{:S(2)}) copy-start(bf16[8192,256]{1,0:T(8,128)(2,1)} %param.8) | copy-start | bytes 12582916
  27.8 1.9 %copy-start = (bf16[128,16384]{1,0:T(8,128)(2,1)}, bf16[128,16384]{1,0:T(8,128)(2,1)S(1)}, u32[]{:S(2)}) copy-start(bf16[128,16384]{1,0:T(8,128)(2,1)S(1)} %constant_dynamic-update-slice_fusion) | copy-start | bytes 12582916
